TPU v7x, 32 devices: a whole 2x2x4 slice. The times are simulated.
32 devices in a mesh: leaf: 8 (over y, x, core), loop: 4 (over z).
Axes of the slice: x: 2, y: 2, z: 4, core: 2. Of those that a mesh axis runs over, the one named last changes fastest.
Arguments:
- jacobian_t: bfloat16 [4, 8192, 512], P('loop', 'leaf'), may hold values from -6 to 6
- leaf_block: bfloat16 [4, 8192, 1024], P('loop', 'leaf'), may hold values from -0.1875 to 0.1875
- left_basis: bfloat16 [4, 8192, 128], P('loop', 'leaf'), may hold values from -0.5 to 0.5
- right_basis: bfloat16 [4, 8192, 128], P('loop', 'leaf'), may hold values from -0.1875 to 0.1875
- couplings: bfloat16 [4, 24, 128, 128], P('loop', 'leaf'), may hold values from -0.5 to 0.5
- group_coupling: bfloat16 [4, 16, 128, 128], P('loop', 'leaf'), may hold values from -0.5 to 0.5
- obs_order: int32 [512], replicated, may hold values from 0 to 511, each once
Outputs:
- cross_cov: bfloat16 [4, 8192, 512], P('loop', 'leaf')
- projected: float32 [512, 512], P('leaf')
Inputs may be any that keep to these rules, and one draw needn't show every extreme that they name: `obs_order`: each observation 0 to 511 appears exactly once.
All inputs are finite; a program needn't handle non-finite values.
Results may differ from a plain program's by a relative error of at most 0.005.
Values sent between devices are 32-bit elements; how exact they have to be, the bound alone decides.
A program may use at most 64 MiB of HBM per device.

v0:
```python
import jax
import jax.numpy as jnp
from jax import lax
from jax.sharding import PartitionSpec as P


def partner(value, axis, stride):
    mask = 2**stride
    pairs = [(source, source ^ mask) for source in range(lax.axis_size(axis))]
    return lax.ppermute(value, axis, pairs)


def from_behind(shard, axis, by):
    devices = lax.axis_size(axis)
    return lax.ppermute(shard, axis, [(i, (i + by) % devices) for i in range(devices)])


def body(jacobian_t, leaf_block, left_basis, right_basis, couplings, group_coupling, obs_order):
    highest = lax.Precision.HIGHEST
    field = jacobian_t[0]
    block = leaf_block[0]
    lefts = left_basis[0]
    rights = right_basis[0]
    coupled = couplings[0].astype(jnp.float32)
    neighbour = group_coupling[0].astype(jnp.float32)
    coef = lax.dot_general(
        rights, field, (((0,), (0,)), ((), ())), preferred_element_type=jnp.float32
    )
    levels = lax.axis_size("leaf").bit_length() - 1
    total = coef
    mixed = jnp.zeros_like(coef)
    for level in range(levels):
        other = partner(total, "leaf", level)
        mixed = mixed + jnp.dot(coupled[level], other, precision=highest)
        total = total + other
    before = from_behind(total, "loop", 1)
    after = from_behind(total, "loop", -1)
    mixed = mixed + jnp.dot(neighbour[0], before, precision=highest)
    mixed = mixed + jnp.dot(neighbour[1], after, precision=highest)
    mixed = mixed.astype(jnp.bfloat16)
    near = jnp.dot(block, field, preferred_element_type=jnp.float32)
    far = jnp.dot(lefts, mixed, preferred_element_type=jnp.float32)
    cross = (near + far).astype(jnp.bfloat16)
    partial_value = lax.dot_general(
        field, cross, (((0,), (0,)), ((), ())), preferred_element_type=jnp.float32
    )
    ordered = partial_value[obs_order]
    mine = lax.psum_scatter(ordered, "leaf", scatter_dimension=0, tiled=True)
    projected = lax.psum(mine, "loop")
    return (cross[None], projected)


def solution(mesh):
    in_specs = (
        P("loop", "leaf", None),
        P("loop", "leaf", None),
        P("loop", "leaf", None),
        P("loop", "leaf", None),
        P("loop", "leaf", None, None),
        P("loop", "leaf", None, None),
        P(),
    )
    out_specs = (P("loop", "leaf", None), P("leaf", None))
    return jax.shard_map(body, mesh=mesh, in_specs=in_specs, out_specs=out_specs, check_vma=False)
```

profile of v0, /device:TPU:0, one launch (start us, length us, event | category | flops | bytes accessed | tf_op | source)
XLA Modules:
  0.0 131.8 jit_solution(6118895068990609260)
XLA Ops:
  7.2 1.8 %fusion.8 = f32[128,512]{1,0:T(8,128)S(1)} fusion(bf16[1,1024,512]{2,1,0:T(8,128)(2,1)} %param.7, bf16[1,1024,128]{2,1,0:T(8,128)(2,1)} %param.10), kind=kOutput, calls=%fused_computation.12 | convolution fusion | flops 134217728 | bytes 1572864 | tf_op jit(solution)/shard_map/dot_general | solution.py:26
  9.0 0.6 collective-permute-start
  9.6 1.2 collective-permute-done
  10.8 2.9 %collective-permute-start.1 = (f32[128,512]{1,0:T(8,128)S(1)}, f32[128,512]{1,0:T(8,128)S(1)}, u32[]{:S(2)}, u32[]{:S(2)}) collective-permute-start(f32[128,512]{1,0:T(8,128)S(1)} %add.40), channel_id=1, source_target_pairs={{0,8},{4,12},{8,0},{12,4},{16,24},{20,28},{24,16},{28,20},{1,9},{5... | collective-permute-start | bytes 786440 | tf_op jit(solution)/shard_map/ppermute | solution.py:10
  13.7 6.6 %collective-permute-done.1 = f32[128,512]{1,0:T(8,128)S(1)} collective-permute-done((f32[128,512]{1,0:T(8,128)S(1)}, f32[128,512]{1,0:T(8,128)S(1)}, u32[]{:S(2)}, u32[]{:S(2)}) %collective-permute-start.1) | collective-permute-done | bytes 262176 | tf_op jit(solution)/shard_map/ppermute | solution.py:10
  20.4 1.8 %collective-permute-start.2 = (f32[128,512]{1,0:T(8,128)S(1)}, f32[128,512]{1,0:T(8,128)S(1)}, u32[]{:S(2)}, u32[]{:S(2)}) collective-permute-start(f32[128,512]{1,0:T(8,128)S(1)} %add.42), channel_id=1, source_target_pairs={{0,16},{4,20},{8,24},{12,28},{16,0},{20,4},{24,8},{28,12},{1,17},{... | collective-permute-start | bytes 786440 | tf_op jit(solution)/shard_map/ppermute | solution.py:10
  22.2 1.2 fusion.1
  23.5 4.7 %collective-permute-done.2 = f32[128,512]{1,0:T(8,128)S(1)} collective-permute-done((f32[128,512]{1,0:T(8,128)S(1)}, f32[128,512]{1,0:T(8,128)S(1)}, u32[]{:S(2)}, u32[]{:S(2)}) %collective-permute-start.2) | collective-permute-done | bytes 262176 | tf_op jit(solution)/shard_map/ppermute | solution.py:10
  28.3 3.6 %collective-permute-start.4 = (f32[128,512]{1,0:T(8,128)S(1)}, f32[128,512]{1,0:T(8,128)S(1)}, u32[]{:S(2)}, u32[]{:S(2)}) collective-permute-start(f32[128,512]{1,0:T(8,128)S(1)} %add.44), channel_id=1, source_target_pairs={{0,3},{1,0},{2,1},{3,2},{4,7},{5,4},{6,5},{7,6},{8,11},{9,8},{10,9... | collective-permute-start | bytes 786440 | tf_op jit(solution)/shard_map/ppermute | solution.py:15
  31.9 0.4 fusion.19
  32.4 0.4 fusion.17
  32.7 5.8 %collective-permute-done.4 = f32[128,512]{1,0:T(8,128)S(1)} collective-permute-done((f32[128,512]{1,0:T(8,128)S(1)}, f32[128,512]{1,0:T(8,128)S(1)}, u32[]{:S(2)}, u32[]{:S(2)}) %collective-permute-start.4) | collective-permute-done | bytes 262176 | tf_op jit(solution)/shard_map/ppermute | solution.py:15
  38.6 0.4 fusion.13
  39.0 3.6 %collective-permute-done.3 = f32[128,512]{1,0:T(8,128)S(1)} collective-permute-done((f32[128,512]{1,0:T(8,128)S(1)}, f32[128,512]{1,0:T(8,128)S(1)}, u32[]{:S(2)}, u32[]{:S(2)}) %collective-permute-start.3) | collective-permute-done | bytes 262176 | tf_op jit(solution)/shard_map/ppermute | solution.py:15
  42.6 0.4 fusion.15
  43.0 0.4 fusion.6
  43.4 0.4 fusion
  43.8 1.0 copy-done.1
  44.8 1.7 %convolution_bitcast_fusion = f32[512,512]{0,1:T(8,128)} fusion(bf16[1024,512]{1,0:T(8,128)(2,1)S(1)} %fusion, bf16[1,1024,512]{2,1,0:T(8,128)(2,1)S(1)} %copy-done.2), kind=kOutput, calls=%fused_computation.5 | convolution fusion | flops 536870912 | bytes 3145728 | tf_op jit(solution)/shard_map/dot_general | solution.py:44
  46.5 1.6 %copy.10 = f32[512,512]{1,0:T(8,128)S(1)} copy(f32[512,512]{0,1:T(8,128)} %convolution_bitcast_fusion) | data formatting | bytes 2097152 | tf_op jit(solution)/shard_map/dot_general | solution.py:44
  48.1 2.3 %gather_fusion = f32[512,512]{1,0:T(8,128)} fusion(f32[512,512]{1,0:T(8,128)S(1)} %copy.10, s32[1024]{0:T(1024)S(1)} %pad_clamp_fusion), kind=kCustom, calls=%fused_computation | custom fusion | bytes 2099200 | tf_op jit(solution)/shard_map/gather | solution.py:47
  50.5 35.9 %reduce-scatter.2.cloned.1.call-done = f32[64,512]{1,0:T(8,128)} async-done(((f32[512,512]{1,0:T(8,128)}), f32[64,512]{1,0:T(8,128)}) %reduce-scatter.2.cloned.1.call-update) | async-done | bytes 131088 | tf_op jit(solution)/shard_map/reduce_scatter | solution.py:48
  86.4 37.0 %all-reduce.2.cloned.1.call-done = f32[64,512]{1,0:T(8,128)} async-done(((f32[64,512]{1,0:T(8,128)}), f32[64,512]{1,0:T(8,128)}) %all-reduce.2.cloned.1.call-update) | async-done | bytes 131088 | tf_op jit(solution)/shard_map/psum | solution.py:49
  123.4 1.6 %copy.13 = f32[64,512]{1,0:T(8,128)} copy(f32[64,512]{1,0:T(8,128)} %all-reduce.2.cloned.1.call-done) | data formatting | bytes 262144
  (23 shorter events, 0.3 us)
Async XLA Ops:
  7.2 15.1 %copy-start = (bf16[1,1024,1024]{2,1,0:T(8,128)(2,1)S(1)}, bf16[1,1024,1024]{2,1,0:T(8,128)(2,1)}, u32[]{:S(2)}) copy-start(bf16[1,1024,1024]{2,1,0:T(8,128)(2,1)} %param.8) | copy-start | bytes 6291460
  7.2 15.0 %copy-start.2 = (bf16[1,1024,512]{2,1,0:T(8,128)(2,1)S(1)}, bf16[1,1024,512]{2,1,0:T(8,128)(2,1)}, u32[]{:S(2)}) copy-start(bf16[1,1024,512]{2,1,0:T(8,128)(2,1)} %param.7) | copy-start | bytes 3145732
  7.2 6.5 %copy-start.6 = (s32[512]{0:T(512)S(1)}, s32[512]{0:T(512)}, u32[]{:S(2)}) copy-start(s32[512]{0:T(512)} %param.13) | copy-start | bytes 6148
  7.2 79.2 %reduce-scatter.2.cloned.1.call-start = ((), (), s32[]{:S(2)}) async-start(), calls=%async_computation.1 | async-start | bytes 1179648 | tf_op jit(solution)/shard_map/reduce_scatter | solution.py:48
  9.0 1.7 %collective-permute-start = (f32[128,512]{1,0:T(8,128)S(1)}, f32[128,512]{1,0:T(8,128)S(1)}, u32[]{:S(2)}, u32[]{:S(2)}) collective-permute-start(f32[128,512]{1,0:T(8,128)S(1)} %fusion.8), channel_id=1, source_target_pairs={{0,4},{4,0},{8,12},{12,8},{16,20},{20,16},{24,28},{28,24},{1,5},{5... | collective-permute-start | bytes 786440 | tf_op jit(solution)/shard_map/ppermute | solution.py:10
  10.8 9.5 %collective-permute-start.1 = (f32[128,512]{1,0:T(8,128)S(1)}, f32[128,512]{1,0:T(8,128)S(1)}, u32[]{:S(2)}, u32[]{:S(2)}) collective-permute-start(f32[128,512]{1,0:T(8,128)S(1)} %add.40), channel_id=1, source_target_pairs={{0,8},{4,12},{8,0},{12,4},{16,24},{20,28},{24,16},{28,20},{1,9},{5... | collective-permute-start | bytes 786440 | tf_op jit(solution)/shard_map/ppermute | solution.py:10
  20.4 11.5 %copy-start.4 = (bf16[1,3,128,128]{3,2,1,0:T(8,128)(2,1)S(1)}, bf16[1,3,128,128]{3,2,1,0:T(8,128)(2,1)}, u32[]{:S(2)}) copy-start(bf16[1,3,128,128]{3,2,1,0:T(8,128)(2,1)} %param.11) | copy-start | bytes 294916
  20.4 18.2 %copy-start.5 = (bf16[1,2,128,128]{3,2,1,0:T(8,128)(2,1)S(1)}, bf16[1,2,128,128]{3,2,1,0:T(8,128)(2,1)}, u32[]{:S(2)}) copy-start(bf16[1,2,128,128]{3,2,1,0:T(8,128)(2,1)} %param.12) | copy-start | bytes 196612
  20.4 7.8 %collective-permute-start.2 = (f32[128,512]{1,0:T(8,128)S(1)}, f32[128,512]{1,0:T(8,128)S(1)}, u32[]{:S(2)}, u32[]{:S(2)}) collective-permute-start(f32[128,512]{1,0:T(8,128)S(1)} %add.42), channel_id=1, source_target_pairs={{0,16},{4,20},{8,24},{12,28},{16,0},{20,4},{24,8},{28,12},{1,17},{... | collective-permute-start | bytes 786440 | tf_op jit(solution)/shard_map/ppermute | solution.py:10
  23.5 19.9 %copy-start.3 = (bf16[1,1024,128]{2,1,0:T(8,128)(2,1)S(1)}, bf16[1,1024,128]{2,1,0:T(8,128)(2,1)}, u32[]{:S(2)}) copy-start(bf16[1,1024,128]{2,1,0:T(8,128)(2,1)} %param.9) | copy-start | bytes 786436
  28.3 10.3 %collective-permute-start.4 = (f32[128,512]{1,0:T(8,128)S(1)}, f32[128,512]{1,0:T(8,128)S(1)}, u32[]{:S(2)}, u32[]{:S(2)}) collective-permute-start(f32[128,512]{1,0:T(8,128)S(1)} %add.44), channel_id=1, source_target_pairs={{0,3},{1,0},{2,1},{3,2},{4,7},{5,4},{6,5},{7,6},{8,11},{9,8},{10,9... | collective-permute-start | bytes 786440 | tf_op jit(solution)/shard_map/ppermute | solution.py:15
  32.3 10.3 %collective-permute-start.3 = (f32[128,512]{1,0:T(8,128)S(1)}, f32[128,512]{1,0:T(8,128)S(1)}, u32[]{:S(2)}, u32[]{:S(2)}) collective-permute-start(f32[128,512]{1,0:T(8,128)S(1)} %add.44), channel_id=1, source_target_pairs={{0,1},{1,2},{2,3},{3,0},{4,5},{5,6},{6,7},{7,4},{8,9},{9,10},{10,1... | collective-permute-start | bytes 786440 | tf_op jit(solution)/shard_map/ppermute | solution.py:15
  43.8 1.0 copy-start.1
  50.4 72.9 %all-reduce.2.cloned.1.call-start = ((), (), s32[]{:S(2)}) async-start(), calls=%async_computation.2 | async-start | bytes 262144 | tf_op jit(solution)/shard_map/psum | solution.py:49
Sparse Core Ops, SparseCore 0:
  50.5 35.7 reduce-scatter.1
  88.7 34.6 all-reduce.1
where the time goes:
time: 132 us
  waiting for transfers between devices  94.8 us (72%)
  between operations  14.2 us (11%)
  starting transfers between devices  9.07 us (7%)
  matrix products  7.13 us (5%)
  local copies, waits for them, and re-layouts  6.45 us (5%)
    psum x1, waiting for transfers between devices, body(): projected = lax.psum(mine, 'loop')  37 us
    reduce_scatter x1, waiting for transfers between devices, body(): mine = lax.psum_scatter(ordered, 'leaf', scatter_dimension=0, tiled=True)  35.9 us
    ppermute x3, waiting for transfers between devices, partner(): return lax.ppermute(value, axis, pairs)  12.5 us
    ppermute x2, waiting for transfers between devices, from_behind(): lax.ppermute(shard, axis, [(i, (i + by) % devices) for i in range(devices)])  9.41 us
    ppermute x3, starting transfers between devices, partner(): return lax.ppermute(value, axis, pairs)  5.31 us
    ppermute x2, starting transfers between devices, from_behind(): lax.ppermute(shard, axis, [(i, (i + by) % devices) for i in range(devices)])  3.68 us
  transfers between devices with their start and end apart: 7, of which 7 were waited for; matrix products, arithmetic and copies ran while one was open for 2% of the time, Pallas kernels for 0%

commit v1 on v0

--- a/solution.py
+++ b/solution.py
@@ -46,7 +46,7 @@
     )
     ordered = partial_value[obs_order]
     mine = lax.psum_scatter(ordered, "leaf", scatter_dimension=0, tiled=True)
-    projected = lax.psum(mine, "loop")
+    projected = jnp.sum(lax.all_gather(mine, "loop"), 0)
     return (cross[None], projected)
 
 

time: 132 us -> 110 us (0.83)
  waiting for transfers between devices: 94.8 us -> 57.9 us
  blocking collectives: 0 us -> 15.6 us
  local copies, waits for them, and re-layouts: 6.45 us -> 4.87 us
    psum x1 -> x0, waiting for transfers between devices: 37 us -> none  [body(): projected = lax.psum(mine, 'loop')]
    all_gather x0 -> x1, blocking collectives: none -> 15.6 us  [body(): projected = jnp.sum(lax.all_gather(mine, 'loop'), 0)]
    unnamed x15 -> x14, local copies, waits for them, and re-layouts: 2.57 us -> 1 us
  transfers between devices with their start and end apart: 7 -> 6, of which waited for: 7 -> 6; matrix products, arithmetic and copies ran while one was open for 2% -> 2% of each run, Pallas kernels for 0% -> 0%
where the time goes in v1:
time: 110 us; the launch traced here: 109 us
  waiting for transfers between devices  57.9 us (53%)
  blocking collectives  15.6 us (14%)
  between operations  14.2 us (13%)
  starting transfers between devices  9.03 us (8%)
  matrix products  7.1 us (6%)
  local copies, waits for them, and re-layouts  4.87 us (4%)
    reduce_scatter x1, waiting for transfers between devices, body(): mine = lax.psum_scatter(ordered, 'leaf', scatter_dimension=0, tiled=True)  36 us
    all_gather x1, blocking collectives, body(): projected = jnp.sum(lax.all_gather(mine, 'loop'), 0)  15.6 us
    ppermute x3, waiting for transfers between devices, partner(): return lax.ppermute(value, axis, pairs)  12.5 us
    ppermute x2, waiting for transfers between devices, from_behind(): lax.ppermute(shard, axis, [(i, (i + by) % devices) for i in range(devices)])  9.41 us
    ppermute x3, starting transfers between devices, partner(): return lax.ppermute(value, axis, pairs)  5.31 us
    ppermute x2, starting transfers between devices, from_behind(): lax.ppermute(shard, axis, [(i, (i + by) % devices) for i in range(devices)])  3.68 us
    gather x1, local copies, waits for them, and re-layouts, body(): ordered = partial_value[obs_order]  2.31 us
  transfers between devices with their start and end apart: 6, of which 6 were waited for; matrix products, arithmetic and copies ran while one was open for 2% of the time, Pallas kernels for 0%

profile of v1, /device:TPU:0, one launch (start us, length us, event | category | flops | bytes accessed | tf_op | source)
XLA Modules:
  0.0 109.5 jit_solution(15772115874556824561)
XLA Ops:
  7.2 1.8 %fusion.8 = f32[128,512]{1,0:T(8,128)S(1)} fusion(bf16[1,1024,512]{2,1,0:T(8,128)(2,1)} %param.7, bf16[1,1024,128]{2,1,0:T(8,128)(2,1)} %param.10), kind=kOutput, calls=%fused_computation.12 | convolution fusion | flops 134217728 | bytes 1572864 | tf_op jit(solution)/shard_map/dot_general | solution.py:26
  9.0 0.6 collective-permute-start
  9.6 1.2 %collective-permute-done = f32[128,512]{1,0:T(8,128)S(1)} collective-permute-done((f32[128,512]{1,0:T(8,128)S(1)}, f32[128,512]{1,0:T(8,128)S(1)}, u32[]{:S(2)}, u32[]{:S(2)}) %collective-permute-start) | collective-permute-done | bytes 262176 | tf_op jit(solution)/shard_map/ppermute | solution.py:10
  10.8 2.9 %collective-permute-start.1 = (f32[128,512]{1,0:T(8,128)S(1)}, f32[128,512]{1,0:T(8,128)S(1)}, u32[]{:S(2)}, u32[]{:S(2)}) collective-permute-start(f32[128,512]{1,0:T(8,128)S(1)} %add.38), channel_id=1, source_target_pairs={{0,8},{4,12},{8,0},{12,4},{16,24},{20,28},{24,16},{28,20},{1,9},{5... | collective-permute-start | bytes 786440 | tf_op jit(solution)/shard_map/ppermute | solution.py:10
  13.7 6.6 %collective-permute-done.1 = f32[128,512]{1,0:T(8,128)S(1)} collective-permute-done((f32[128,512]{1,0:T(8,128)S(1)}, f32[128,512]{1,0:T(8,128)S(1)}, u32[]{:S(2)}, u32[]{:S(2)}) %collective-permute-start.1) | collective-permute-done | bytes 262176 | tf_op jit(solution)/shard_map/ppermute | solution.py:10
  20.4 1.8 %collective-permute-start.2 = (f32[128,512]{1,0:T(8,128)S(1)}, f32[128,512]{1,0:T(8,128)S(1)}, u32[]{:S(2)}, u32[]{:S(2)}) collective-permute-start(f32[128,512]{1,0:T(8,128)S(1)} %add.40), channel_id=1, source_target_pairs={{0,16},{4,20},{8,24},{12,28},{16,0},{20,4},{24,8},{28,12},{1,17},{... | collective-permute-start | bytes 786440 | tf_op jit(solution)/shard_map/ppermute | solution.py:10
  22.2 1.2 %fusion.1 = f32[1024,512]{1,0:T(8,128)S(1)} fusion(bf16[1,1024,1024]{2,1,0:T(8,128)(2,1)S(1)} %copy-done, bf16[1,1024,512]{2,1,0:T(8,128)(2,1)S(1)} %copy-done.2), kind=kOutput, calls=%fused_computation.3 | convolution fusion | flops 1073741824 | bytes 5242880 | tf_op jit(solution)/shard_map/dot_general | solution.py:41
  23.5 4.7 %collective-permute-done.2 = f32[128,512]{1,0:T(8,128)S(1)} collective-permute-done((f32[128,512]{1,0:T(8,128)S(1)}, f32[128,512]{1,0:T(8,128)S(1)}, u32[]{:S(2)}, u32[]{:S(2)}) %collective-permute-start.2) | collective-permute-done | bytes 262176 | tf_op jit(solution)/shard_map/ppermute | solution.py:10
  28.3 3.6 %collective-permute-start.4 = (f32[128,512]{1,0:T(8,128)S(1)}, f32[128,512]{1,0:T(8,128)S(1)}, u32[]{:S(2)}, u32[]{:S(2)}) collective-permute-start(f32[128,512]{1,0:T(8,128)S(1)} %add.42), channel_id=1, source_target_pairs={{0,3},{1,0},{2,1},{3,2},{4,7},{5,4},{6,5},{7,6},{8,11},{9,8},{10,9... | collective-permute-start | bytes 786440 | tf_op jit(solution)/shard_map/ppermute | solution.py:15
  31.9 0.4 fusion.19
  32.3 0.4 fusion.17
  32.7 5.8 %collective-permute-done.4 = f32[128,512]{1,0:T(8,128)S(1)} collective-permute-done((f32[128,512]{1,0:T(8,128)S(1)}, f32[128,512]{1,0:T(8,128)S(1)}, u32[]{:S(2)}, u32[]{:S(2)}) %collective-permute-start.4) | collective-permute-done | bytes 262176 | tf_op jit(solution)/shard_map/ppermute | solution.py:15
  38.6 0.4 fusion.13
  39.0 3.6 %collective-permute-done.3 = f32[128,512]{1,0:T(8,128)S(1)} collective-permute-done((f32[128,512]{1,0:T(8,128)S(1)}, f32[128,512]{1,0:T(8,128)S(1)}, u32[]{:S(2)}, u32[]{:S(2)}) %collective-permute-start.3) | collective-permute-done | bytes 262176 | tf_op jit(solution)/shard_map/ppermute | solution.py:15
  42.6 0.4 fusion.15
  43.0 0.4 fusion.6
  43.4 0.4 fusion
  43.8 1.0 copy-done.1
  44.8 1.7 %convolution_bitcast_fusion = f32[512,512]{0,1:T(8,128)} fusion(bf16[1024,512]{1,0:T(8,128)(2,1)S(1)} %fusion, bf16[1,1024,512]{2,1,0:T(8,128)(2,1)S(1)} %copy-done.2), kind=kOutput, calls=%fused_computation.5 | convolution fusion | flops 536870912 | bytes 3145728 | tf_op jit(solution)/shard_map/dot_general | solution.py:44
  46.5 1.6 %copy.10 = f32[512,512]{1,0:T(8,128)S(1)} copy(f32[512,512]{0,1:T(8,128)} %convolution_bitcast_fusion) | data formatting | bytes 2097152 | tf_op jit(solution)/shard_map/dot_general | solution.py:44
  48.0 2.3 %gather_fusion = f32[512,512]{1,0:T(8,128)} fusion(f32[512,512]{1,0:T(8,128)S(1)} %copy.10, s32[1024]{0:T(1024)S(1)} %pad_clamp_fusion), kind=kCustom, calls=%fused_computation | custom fusion | bytes 2099200 | tf_op jit(solution)/shard_map/gather | solution.py:47
  50.4 36.0 %reduce-scatter.2.cloned.1.call-done = f32[64,512]{1,0:T(8,128)} async-done(((f32[512,512]{1,0:T(8,128)}), f32[64,512]{1,0:T(8,128)}) %reduce-scatter.2.cloned.1.call-update) | async-done | bytes 131088 | tf_op jit(solution)/shard_map/reduce_scatter | solution.py:48
  86.3 15.6 %all-gather = f32[256,512]{1,0:T(8,128)S(1)} all-gather(f32[64,512]{1,0:T(8,128)} %reduce-scatter.2.cloned.1.call-done), channel_id=2, replica_groups=mesh['leaf'=8,'loop'=4] {'loop'}, dimensions={0}, use_global_device_ids=true | all-gather | bytes 655360 | tf_op jit(solution)/shard_map/all_gather | solution.py:49
  101.9 0.7 reduce_sum.9
  (21 shorter events, 0.3 us)
Async XLA Ops:
  7.2 15.1 %copy-start = (bf16[1,1024,1024]{2,1,0:T(8,128)(2,1)S(1)}, bf16[1,1024,1024]{2,1,0:T(8,128)(2,1)}, u32[]{:S(2)}) copy-start(bf16[1,1024,1024]{2,1,0:T(8,128)(2,1)} %param.8) | copy-start | bytes 6291460
  7.2 15.0 %copy-start.2 = (bf16[1,1024,512]{2,1,0:T(8,128)(2,1)S(1)}, bf16[1,1024,512]{2,1,0:T(8,128)(2,1)}, u32[]{:S(2)}) copy-start(bf16[1,1024,512]{2,1,0:T(8,128)(2,1)} %param.7) | copy-start | bytes 3145732
  7.2 6.5 %copy-start.6 = (s32[512]{0:T(512)S(1)}, s32[512]{0:T(512)}, u32[]{:S(2)}) copy-start(s32[512]{0:T(512)} %param.13) | copy-start | bytes 6148
  7.2 79.1 %reduce-scatter.2.cloned.1.call-start = ((), (), s32[]{:S(2)}) async-start(), calls=%async_computation.1 | async-start | bytes 1179648 | tf_op jit(solution)/shard_map/reduce_scatter | solution.py:48
  9.0 1.7 %collective-permute-start = (f32[128,512]{1,0:T(8,128)S(1)}, f32[128,512]{1,0:T(8,128)S(1)}, u32[]{:S(2)}, u32[]{:S(2)}) collective-permute-start(f32[128,512]{1,0:T(8,128)S(1)} %fusion.8), channel_id=1, source_target_pairs={{0,4},{4,0},{8,12},{12,8},{16,20},{20,16},{24,28},{28,24},{1,5},{5... | collective-permute-start | bytes 786440 | tf_op jit(solution)/shard_map/ppermute | solution.py:10
  10.8 9.5 %collective-permute-start.1 = (f32[128,512]{1,0:T(8,128)S(1)}, f32[128,512]{1,0:T(8,128)S(1)}, u32[]{:S(2)}, u32[]{:S(2)}) collective-permute-start(f32[128,512]{1,0:T(8,128)S(1)} %add.38), channel_id=1, source_target_pairs={{0,8},{4,12},{8,0},{12,4},{16,24},{20,28},{24,16},{28,20},{1,9},{5... | collective-permute-start | bytes 786440 | tf_op jit(solution)/shard_map/ppermute | solution.py:10
  20.4 11.5 %copy-start.4 = (bf16[1,3,128,128]{3,2,1,0:T(8,128)(2,1)S(1)}, bf16[1,3,128,128]{3,2,1,0:T(8,128)(2,1)}, u32[]{:S(2)}) copy-start(bf16[1,3,128,128]{3,2,1,0:T(8,128)(2,1)} %param.11) | copy-start | bytes 294916
  20.4 18.2 %copy-start.5 = (bf16[1,2,128,128]{3,2,1,0:T(8,128)(2,1)S(1)}, bf16[1,2,128,128]{3,2,1,0:T(8,128)(2,1)}, u32[]{:S(2)}) copy-start(bf16[1,2,128,128]{3,2,1,0:T(8,128)(2,1)} %param.12) | copy-start | bytes 196612
  20.4 7.8 %collective-permute-start.2 = (f32[128,512]{1,0:T(8,128)S(1)}, f32[128,512]{1,0:T(8,128)S(1)}, u32[]{:S(2)}, u32[]{:S(2)}) collective-permute-start(f32[128,512]{1,0:T(8,128)S(1)} %add.40), channel_id=1, source_target_pairs={{0,16},{4,20},{8,24},{12,28},{16,0},{20,4},{24,8},{28,12},{1,17},{... | collective-permute-start | bytes 786440 | tf_op jit(solution)/shard_map/ppermute | solution.py:10
  23.5 19.9 %copy-start.3 = (bf16[1,1024,128]{2,1,0:T(8,128)(2,1)S(1)}, bf16[1,1024,128]{2,1,0:T(8,128)(2,1)}, u32[]{:S(2)}) copy-start(bf16[1,1024,128]{2,1,0:T(8,128)(2,1)} %param.9) | copy-start | bytes 786436
  28.3 10.3 %collective-permute-start.4 = (f32[128,512]{1,0:T(8,128)S(1)}, f32[128,512]{1,0:T(8,128)S(1)}, u32[]{:S(2)}, u32[]{:S(2)}) collective-permute-start(f32[128,512]{1,0:T(8,128)S(1)} %add.42), channel_id=1, source_target_pairs={{0,3},{1,0},{2,1},{3,2},{4,7},{5,4},{6,5},{7,6},{8,11},{9,8},{10,9... | collective-permute-start | bytes 786440 | tf_op jit(solution)/shard_map/ppermute | solution.py:15
  32.3 10.3 %collective-permute-start.3 = (f32[128,512]{1,0:T(8,128)S(1)}, f32[128,512]{1,0:T(8,128)S(1)}, u32[]{:S(2)}, u32[]{:S(2)}) collective-permute-start(f32[128,512]{1,0:T(8,128)S(1)} %add.42), channel_id=1, source_target_pairs={{0,1},{1,2},{2,3},{3,0},{4,5},{5,6},{6,7},{7,4},{8,9},{9,10},{10,1... | collective-permute-start | bytes 786440 | tf_op jit(solution)/shard_map/ppermute | solution.py:15
  43.8 1.0 copy-start.1
Sparse Core Ops, SparseCore 0:
  50.5 35.7 reduce-scatter.1
